TPU v7x, 128 devices: a whole 4x4x4 slice. The times are simulated.
128 devices in a mesh: clus: 8 (over x, core), trow: 4 (over y), tcol: 4 (over z).
Axes of the slice: x: 4, y: 4, z: 4, core: 2. Of those that a mesh axis runs over, the one named last changes fastest.
Arguments:
- embeddings: bfloat16 [65536, 1024], P(('clus', 'trow', 'tcol'))
- target: int32 [65536], P(('clus', 'trow', 'tcol')), may hold values from 0 to 98303, as said below
Outputs:
- best_cosine: float32 [65536], P(('clus', 'trow', 'tcol'))
Inputs may be any that keep to these rules, and one draw needn't show every extreme that they name: `target`: the grid has 8 clusters of 12288 slots each; the rows of a cluster fill its slots 0 to its size - 1, each slot once; every cluster has a row, and the last cluster is the largest and fills all 12288 slots. The rows of one device send at most 6 rows to any aligned block of 768 slots, and some block receives exactly 6 from every device.
All inputs are finite; a program needn't handle non-finite values.
Results may differ from a plain program's by a relative error of at most 0.00069.
Values may be sent and summed in bfloat16 or wider, within the bound.
A program may use at most 128 MiB of HBM per device.

v0:
```python
import jax
import jax.numpy as jnp
from jax import lax
from jax.sharding import PartitionSpec as P

SLOTS = 768


epsilon = 1e-06


def compare(left_rows, left_index, pieces, column_index):
    scores = lax.dot_general(
        left_rows, pieces[0], (((1,), (1,)), ((), ())), preferred_element_type=jnp.float32
    )
    keep = (pieces[1][None, :] > 0) & (column_index[None, :] != left_index[:, None])
    return jnp.max(jnp.where(keep, scores, -1.0), axis=1)


def on_device(embeddings, target):
    width = embeddings.shape[1]
    clusters_count = lax.axis_size("clus")
    tile_rows = lax.axis_size("trow")
    tile_cols = lax.axis_size("tcol")
    group_count = tile_rows * tile_cols
    devices = clusters_count * group_count
    pair_rows = SLOTS // devices
    destination = target // SLOTS
    onehot = (destination[:, None] == jnp.arange(devices, dtype=jnp.int32)[None, :]).astype(
        jnp.int32
    )
    position = jnp.sum(onehot * (jnp.cumsum(onehot, axis=0) - 1), axis=1)
    buffer_slot = destination * pair_rows + position
    outgoing = jnp.zeros((SLOTS, width), jnp.bfloat16).at[buffer_slot].set(embeddings)
    markers = jnp.zeros((SLOTS,), jnp.bfloat16).at[buffer_slot].set(1.0)
    arrived, present = (
        lax.all_to_all(
            outgoing.reshape(devices, pair_rows, width),
            ("clus", "trow", "tcol"),
            split_axis=0,
            concat_axis=0,
            tiled=True,
        ),
        lax.all_to_all(
            markers.reshape(devices, pair_rows),
            ("clus", "trow", "tcol"),
            split_axis=0,
            concat_axis=0,
            tiled=True,
        ),
    )
    arrived = arrived.reshape(SLOTS, width)
    present = present.reshape(SLOTS)
    values = arrived.astype(jnp.float32)
    unit_rows = (
        values / jnp.sqrt(jnp.sum(values * values, axis=1, keepdims=True) + epsilon)
    ).astype(jnp.bfloat16)
    row_pos = lax.axis_index("trow")
    col_pos = lax.axis_index("tcol")
    own_index = (row_pos * tile_cols + col_pos) * SLOTS + jnp.arange(SLOTS, dtype=jnp.int32)
    pieces = (
        lax.all_gather(unit_rows, ("trow", "tcol"), axis=0, tiled=True),
        lax.all_gather(present, ("trow", "tcol"), axis=0, tiled=True),
    )
    column_index = jnp.arange(pieces[0].shape[0], dtype=jnp.int32)
    best = jnp.maximum(
        jnp.full((SLOTS,), -1.0, jnp.float32), compare(unit_rows, own_index, pieces, column_index)
    )
    returned = lax.all_to_all(
        best.reshape(devices, pair_rows),
        ("clus", "trow", "tcol"),
        split_axis=0,
        concat_axis=0,
        tiled=True,
    )
    return returned.reshape(SLOTS)[buffer_slot]


def solution(mesh):
    in_specs = (P(("clus", "trow", "tcol"), None), P(("clus", "trow", "tcol")))
    out_specs = P(("clus", "trow", "tcol"))
    return jax.shard_map(
        on_device, mesh=mesh, in_specs=in_specs, out_specs=out_specs, check_vma=False
    )
```

profile of v0, /device:TPU:1, one launch (start us, length us, event | category | flops | bytes accessed | tf_op | source)
XLA Modules:
  0.0 270.4 jit_solution(13264112457316869931)
XLA Ops:
  6.5 0.0 all-gather.3.cloned.1.call-start
  6.5 0.7 fusion.12
  7.2 0.7 add_select_fusion
  7.9 0.1 copy.5
  8.0 0.2 fusion.4
  8.3 0.1 add_add_fusion
  8.4 0.2 fusion.3
  8.6 0.7 compare_select_fusion
  9.3 3.7 %scatter_custom_fusion.1 = bf16[768,1024]{1,0:T(8,128)(2,1)S(1)} fusion(s32[512]{0:T(512)S(1)} %compare_select_fusion, bf16[512,1024]{1,0:T(8,128)(2,1)} %param.2, bf16[]{:T(256)} %constant.14.clone.1), kind=kCustom, calls=%fused_computation.8 | custom fusion | bytes 1573376 | tf_op jit(solution)/shard_map/scatter | solution.py:34
  13.0 1.6 reshape.73
  14.6 40.8 %all_to_all.21 = bf16[128,6,1024]{2,1,0:T(8,128)(2,1)S(1)} all-to-all(bf16[128,6,1024]{2,1,0:T(8,128)(2,1)} %reshape.73), channel_id=1, replica_groups=mesh['clus'=8,'trow'=4,'tcol'=4] {'clus','trow','tcol'}, dimensions={0} | all-to-all | bytes 3145728 | tf_op jit(solution)/shard_map/all_to_all | solution.py:37
  55.5 0.6 multiply_reduce_fusion
  56.1 0.1 sqrt.12
  56.3 1.9 reshape.75
  58.2 3.5 %divide_convert_fusion = bf16[768,1024]{1,0:T(8,128)(2,1)} fusion(f32[768,1024]{1,0:T(8,128)} %reshape.75, f32[768]{0:T(1024)S(1)} %sqrt.12), kind=kLoop, calls=%fused_computation.7 | loop fusion | flops 1572864 | bytes 4721664 | tf_op jit(solution)/shard_map/convert_element_type | solution.py:57
  61.7 0.0 all-gather.3.cloned.1.call-update
  61.7 3.8 %scatter_custom_fusion = bf16[768]{0:T(1024)(128)(2,1)S(1)} fusion(s32[512]{0:T(512)S(1)} %compare_select_fusion, bf16[512]{0:T(512)(128)(2,1)S(1)} %broadcast.54, bf16[]{:T(256)} %constant.14.clone.1), kind=kCustom, calls=%fused_computation.29 | custom fusion | bytes 1538 | tf_op jit(solution)/shard_map/scatter | solution.py:35
  65.5 0.8 all_to_all.17
  66.3 5.0 %all-to-all-start = ((bf16[128,1,6]{2,1,0:T(2,128)(2,1)}), bf16[128,1,6]{2,1,0:T(2,128)(2,1)S(1)}, u32[]{:S(2)}, u32[]{:S(2)}) async-start(bf16[128,1,6]{2,1,0:T(2,128)(2,1)} %all_to_all.17), calls=%async_computation | async-start | bytes 131072 | tf_op jit(solution)/shard_map/all_to_all | solution.py:44
  71.3 9.6 %all-to-all-done = bf16[128,1,6]{2,1,0:T(2,128)(2,1)S(1)} async-done(((bf16[128,1,6]{2,1,0:T(2,128)(2,1)}), bf16[128,1,6]{2,1,0:T(2,128)(2,1)S(1)}, u32[]{:S(2)}, u32[]{:S(2)}) %all-to-all-start) | async-done | bytes 1568 | tf_op jit(solution)/shard_map/all_to_all | solution.py:44
  80.9 0.2 reduce.1
  81.1 0.1 reshape.103
  81.3 19.5 %all-gather = bf16[16,1,768]{2,1,0:T(2,128)(2,1)S(1)} all-gather(bf16[1,1,768]{2,1,0:T(2,128)(2,1)S(1)} %reshape.103), channel_id=1, replica_groups=mesh['clus'=8,'trow'=4,'tcol'=4] {'trow','tcol'}, dimensions={0}, use_global_device_ids=true | all-gather | bytes 26112 | tf_op jit(solution)/shard_map/all_gather | solution.py:63
  100.8 0.2 compare_reduce_fusion
  101.0 112.6 %all-gather.3.cloned.1.call-done = bf16[12288,1024]{1,0:T(8,128)(2,1)} async-done(((bf16[768,1024]{1,0:T(8,128)(2,1)}), bf16[12288,1024]{1,0:T(8,128)(2,1)}) %all-gather.3.cloned.1.call-update) | async-done | bytes 25165840 | tf_op jit(solution)/shard_map/all_gather | solution.py:62
  213.6 26.6 %select_reduce_fusion = f32[768]{0:T(1024)S(1)} fusion(bf16[768,1024]{1,0:T(8,128)(2,1)} %divide_convert_fusion, bf16[12288,1024]{1,0:T(8,128)(2,1)} %all-gather.3.cloned.1.call-done, s32[768]{0:T(1024)S(1)} %iota_add_fusion, pred[12288]{0:T(1024)(128)(4,1)S(1)} %reshape.106), kind=kOutput, calls=%fused_computation.3 | convolution fusion | flops 19365101568 | bytes 26757120 | tf_op jit(solution)/shard_map/dot_general | solution.py:13
  240.3 0.8 max_broadcast_in_dim.15
  241.0 8.0 %all-to-all-start.2 = ((f32[128,1,6]{2,1,0:T(1,128)}), f32[128,1,6]{2,1,0:T(1,128)S(1)}, u32[]{:S(2)}, u32[]{:S(2)}) async-start(f32[128,1,6]{2,1,0:T(1,128)} %bitcast.4), calls=%async_computation.2 | async-start | bytes 131072 | tf_op jit(solution)/shard_map/all_to_all | solution.py:69
  249.1 9.6 %all-to-all-done.2 = f32[128,1,6]{2,1,0:T(1,128)S(1)} async-done(((f32[128,1,6]{2,1,0:T(1,128)}), f32[128,1,6]{2,1,0:T(1,128)S(1)}, u32[]{:S(2)}, u32[]{:S(2)}) %all-to-all-start.2) | async-done | bytes 3104 | tf_op jit(solution)/shard_map/all_to_all | solution.py:69
  258.7 0.5 broadcast.71
  259.2 0.8 reduce.7
  260.0 0.1 reshape.74
  260.1 3.4 %gather_fusion = f32[512]{0:T(512)} fusion(f32[768]{0:T(1024)S(1)} %reshape.74, s32[1024]{0:T(1024)S(1)} %pad_clamp_fusion), kind=kCustom, calls=%fused_computation | custom fusion | bytes 6144 | tf_op jit(solution)/shard_map/gather | solution.py:76
  (10 shorter events, 0.1 us)
Async XLA Ops:
  6.5 207.1 %all-gather.3.cloned.1.call-start = ((), (), s32[]{:S(2)}) async-start(), calls=%async_computation.3 | async-start | bytes 26738688 | tf_op jit(solution)/shard_map/all_gather | solution.py:62
  66.3 14.6 %all-to-all-start = ((bf16[128,1,6]{2,1,0:T(2,128)(2,1)}), bf16[128,1,6]{2,1,0:T(2,128)(2,1)S(1)}, u32[]{:S(2)}, u32[]{:S(2)}) async-start(bf16[128,1,6]{2,1,0:T(2,128)(2,1)} %all_to_all.17), calls=%async_computation | async-start | bytes 131072 | tf_op jit(solution)/shard_map/all_to_all | solution.py:44
  241.0 17.6 %all-to-all-start.2 = ((f32[128,1,6]{2,1,0:T(1,128)}), f32[128,1,6]{2,1,0:T(1,128)S(1)}, u32[]{:S(2)}, u32[]{:S(2)}) async-start(f32[128,1,6]{2,1,0:T(1,128)} %bitcast.4), calls=%async_computation.2 | async-start | bytes 131072 | tf_op jit(solution)/shard_map/all_to_all | solution.py:69
Sparse Core Ops, SparseCore 0:
  61.8 151.7 all-gather.2
where the time goes:
time: 271 us; the launch traced here: 270 us
  waiting for transfers between devices  132 us (49%)
  blocking collectives  60.4 us (22%)
  matrix products  26.6 us (10%)
  local copies, waits for them, and re-layouts  17 us (6%)
  between operations  13.5 us (5%)
  starting transfers between devices  13.1 us (5%)
  other arithmetic  7.94 us (3%)
    all_gather x1, waiting for transfers between devices, on_device(): lax.all_gather(unit_rows, ('trow', 'tcol'), axis=0, tiled=True)  113 us
    all_to_all x1, blocking collectives, on_device(): lax.all_to_all(outgoing.reshape(devices, pair_rows, width), ('clus', 'tro...  40.8 us
    dot_general x1, matrix products, compare(): lax.dot_general(left_rows, pieces[0], (((1,), (1,)), ((), ())), preferred...  26.6 us
    all_gather x1, blocking collectives, on_device(): lax.all_gather(present, ('trow', 'tcol'), axis=0, tiled=True)  19.5 us
    all_to_all x1, waiting for transfers between devices, on_device(): lax.all_to_all(best.reshape(devices, pair_rows), ('clus', 'trow', 'tcol')...  9.59 us
    all_to_all x1, waiting for transfers between devices, on_device(): lax.all_to_all(markers.reshape(devices, pair_rows), ('clus', 'trow', 'tco...  9.58 us
    all_to_all x1, starting transfers between devices, on_device(): lax.all_to_all(best.reshape(devices, pair_rows), ('clus', 'trow', 'tcol')...  8.03 us
  transfers between devices with their start and end apart: 3, of which 3 were waited for; matrix products, arithmetic and copies ran while one was open for 2% of the time, Pallas kernels for 0%

commit v1 on v0

v1 whole, which is shorter than its diff:
```python
import jax
import jax.numpy as jnp
from jax import lax
from jax.sharding import PartitionSpec as P

SLOTS = 768

epsilon = 1e-06
ABSENT = 4.0


def on_device(embeddings, target):
    width = embeddings.shape[1]
    clusters_count = lax.axis_size("clus")
    tile_rows = lax.axis_size("trow")
    tile_cols = lax.axis_size("tcol")
    group_count = tile_rows * tile_cols
    devices = clusters_count * group_count
    pair_rows = SLOTS // devices

    values = embeddings.astype(jnp.float32)
    unit_rows = (
        values / jnp.sqrt(jnp.sum(values * values, axis=1, keepdims=True) + epsilon)
    ).astype(jnp.bfloat16)

    destination = target // SLOTS
    onehot = (destination[:, None] == jnp.arange(devices, dtype=jnp.int32)[None, :]).astype(
        jnp.int32
    )
    position = jnp.sum(onehot * (jnp.cumsum(onehot, axis=0) - 1), axis=1)
    buffer_slot = destination * pair_rows + position
    outgoing = jnp.full((SLOTS, width), ABSENT, jnp.bfloat16).at[buffer_slot].set(unit_rows)
    arrived = lax.all_to_all(
        outgoing.reshape(devices, pair_rows, width),
        ("clus", "trow", "tcol"),
        split_axis=0,
        concat_axis=0,
        tiled=True,
    ).reshape(SLOTS, width)

    row_pos = lax.axis_index("trow")
    col_pos = lax.axis_index("tcol")
    row_block = lax.all_gather(arrived, "tcol", axis=0, tiled=True)
    col_block = lax.all_gather(arrived, "trow", axis=0, tiled=True)
    local = jnp.arange(SLOTS, dtype=jnp.int32)
    row_index = (
        (row_pos * tile_cols + jnp.arange(tile_cols, dtype=jnp.int32))[:, None] * SLOTS
        + local[None, :]
    ).reshape(-1)
    col_index = (
        (jnp.arange(tile_rows, dtype=jnp.int32) * tile_cols + col_pos)[:, None] * SLOTS
        + local[None, :]
    ).reshape(-1)
    present = col_block[:, 0].astype(jnp.float32) < 2.0
    scores = lax.dot_general(
        row_block, col_block, (((1,), (1,)), ((), ())), preferred_element_type=jnp.float32
    )
    keep = present[None, :] & (col_index[None, :] != row_index[:, None])
    partial = jnp.max(jnp.where(keep, scores, -1.0), axis=1)

    outbound = partial.reshape(tile_cols, devices, pair_rows).transpose(1, 0, 2)
    returned = lax.all_to_all(
        outbound,
        ("clus", "trow", "tcol"),
        split_axis=0,
        concat_axis=0,
        tiled=True,
    )
    best = jnp.max(
        returned.reshape(clusters_count, tile_rows, tile_cols, tile_cols, pair_rows), axis=2
    ).reshape(SLOTS)
    return best[buffer_slot]


def solution(mesh):
    in_specs = (P(("clus", "trow", "tcol"), None), P(("clus", "trow", "tcol")))
    out_specs = P(("clus", "trow", "tcol"))
    return jax.shard_map(
        on_device, mesh=mesh, in_specs=in_specs, out_specs=out_specs, check_vma=False
    )
```

time: 271 us -> 250 us (0.923)
  blocking collectives: 60.4 us -> 40.8 us
  waiting for transfers between devices: 132 us -> 140 us
  local copies, waits for them, and re-layouts: 17 us -> 11 us
  starting transfers between devices: 13.1 us -> 8.98 us
    all_gather x1 -> x0, blocking collectives: 19.5 us -> none  [on_device(): lax.all_gather(present, ('trow', 'tcol'), axis=0, tiled=True)]
    all_gather x1 -> x2, waiting for transfers between devices: 113 us -> 128 us  [the longest x1 66.6 us: on_device(): row_block = lax.all_gather(arrived, 'tcol', axis=0, tiled=True)]
    all_to_all x2 -> x1, waiting for transfers between devices: 19.2 us -> 11.2 us  [on_device(): lax.all_to_all(outbound, ('clus', 'trow', 'tcol'), split_axis=0, concat_a...]
    scatter x2 -> x0, local copies, waits for them, and re-layouts: 7.45 us -> none  [the longest x1 3.77 us: on_device(): markers = jnp.zeros((SLOTS,), jnp.bfloat16).at[buffer_slot].set(1.0)]
    scatter x0 -> x1, other arithmetic: none -> 4.59 us  [on_device(): jnp.full((SLOTS, width), ABSENT, jnp.bfloat16).at[buffer_slot]]
    all_to_all x2 -> x1, starting transfers between devices: 13.1 us -> 8.94 us  [on_device(): lax.all_to_all(outbound, ('clus', 'trow', 'tcol'), split_axis=0, concat_a...]
    reshape x1 -> x3, local copies, waits for them, and re-layouts: 0.13 us -> 4.05 us  [the longest x1 3.7 us: on_device(): arrived = lax.all_to_all(outgoing.reshape(devices, pair_rows, width), ('c...]
    convert_element_type x1 -> x0, other arithmetic: 3.53 us -> none  [on_device(): unit_rows = (values / jnp.sqrt(jnp.sum(values * values, axis=1, keepdims=...]
  transfers between devices with their start and end apart: 3 -> 3, of which waited for: 3 -> 3; matrix products, arithmetic and copies ran while one was open for 2% -> 1% of each run, Pallas kernels for 0% -> 0%
where the time goes in v1:
time: 250 us
  waiting for transfers between devices  140 us (56%)
  blocking collectives  40.8 us (16%)
  matrix products  25.1 us (10%)
  between operations  13.5 us (5%)
  local copies, waits for them, and re-layouts  11 us (4%)
  other arithmetic  10.6 us (4%)
  starting transfers between devices  8.98 us (4%)
    all_gather x1, waiting for transfers between devices, on_device(): row_block = lax.all_gather(arrived, 'tcol', axis=0, tiled=True)  66.6 us
    all_gather x1, waiting for transfers between devices, on_device(): col_block = lax.all_gather(arrived, 'trow', axis=0, tiled=True)  61.4 us
    all_to_all x1, blocking collectives, on_device(): lax.all_to_all(outgoing.reshape(devices, pair_rows, width), ('clus', 'tro...  40.8 us
    dot_general x1, matrix products, on_device(): lax.dot_general(row_block, col_block, (((1,), (1,)), ((), ())), preferred...  25.1 us
    all_to_all x1, waiting for transfers between devices, on_device(): lax.all_to_all(outbound, ('clus', 'trow', 'tcol'), split_axis=0, concat_a...  11.2 us
    all_to_all x1, starting transfers between devices, on_device(): lax.all_to_all(outbound, ('clus', 'trow', 'tcol'), split_axis=0, concat_a...  8.94 us
  transfers between devices with their start and end apart: 3, of which 3 were waited for; matrix products, arithmetic and copies ran while one was open for 1% of the time, Pallas kernels for 0%

profile of v1, /device:TPU:1, one launch (start us, length us, event | category | flops | bytes accessed | tf_op | source)
XLA Modules:
  0.0 249.8 jit_solution(1314348164494295271)
XLA Ops:
  6.5 0.0 all-gather.3.cloned.1.call-start
  6.5 0.7 fusion.14
  7.2 0.7 add_select_fusion
  7.9 0.1 copy.5
  8.0 0.2 fusion.8
  8.3 0.1 add_add_fusion
  8.4 0.2 fusion.7
  8.6 0.7 compare_select_fusion
  9.3 1.5 fusion
  10.8 4.6 %scatter_custom_fusion = bf16[768,1024]{1,0:T(8,128)(2,1)} fusion(s32[512]{0:T(512)S(1)} %compare_select_fusion, bf16[512,1024]{1,0:T(8,128)(2,1)} %param.2, f32[512]{0:T(512)S(1)} %add_sqrt_fusion, bf16[]{:T(256)} %constant.14.clone.1), kind=kCustom, calls=%fused_computation.9 | custom fusion | flops 1572864 | bytes 2623490 | tf_op jit(solution)/shard_map/scatter | solution.py:32
  15.4 2.5 reshape.90
  17.9 40.8 %all_to_all.10 = bf16[128,6,1024]{2,1,0:T(8,128)(2,1)} all-to-all(bf16[128,6,1024]{2,1,0:T(8,128)(2,1)S(1)} %reshape.90), channel_id=1, replica_groups=mesh['clus'=8,'trow'=4,'tcol'=4] {'clus','trow','tcol'}, dimensions={0} | all-to-all | bytes 3145728 | tf_op jit(solution)/shard_map/all_to_all | solution.py:33
  58.7 3.7 %reshape.91 = bf16[768,1024]{1,0:T(8,128)(2,1)} reshape(bf16[128,6,1024]{2,1,0:T(8,128)(2,1)} %all_to_all.10) | data formatting | bytes 3145728 | tf_op jit(solution)/shard_map/reshape | solution.py:39
  62.4 0.0 all-gather.3.cloned.1.call-update
  62.4 0.0 all-gather.5.cloned.1.call-start
  62.4 0.7 all-gather.5.cloned.1.call-update
  63.2 0.1 iota_add_fusion
  63.2 0.1 iota_add_fusion.1
  63.3 61.4 %all-gather.3.cloned.1.call-done = bf16[3072,1024]{1,0:T(8,128)(2,1)} async-done(((bf16[768,1024]{1,0:T(8,128)(2,1)}), bf16[3072,1024]{1,0:T(8,128)(2,1)}) %all-gather.3.cloned.1.call-update) | async-done | bytes 6291472 | tf_op jit(solution)/shard_map/all_gather | solution.py:44
  124.8 1.6 fusion.2
  126.4 66.6 %all-gather.5.cloned.1.call-done = bf16[3072,1024]{1,0:T(8,128)(2,1)} async-done(((bf16[768,1024]{1,0:T(8,128)(2,1)}), bf16[3072,1024]{1,0:T(8,128)(2,1)}) %all-gather.5.cloned.1.call-update) | async-done | bytes 6291472 | tf_op jit(solution)/shard_map/all_gather | solution.py:43
  193.0 25.1 %select_reduce_fusion = f32[3072]{0:T(1024)S(1)} fusion(bf16[3072,1024]{1,0:T(8,128)(2,1)} %all-gather.5.cloned.1.call-done, bf16[3072,1024]{1,0:T(8,128)(2,1)} %all-gather.3.cloned.1.call-done, s32[3072]{0:T(1024)S(1)} %add.97, s32[3072]{0:T(1024)S(1)} %add.91, pred[3072]{0:T(1024)(128)(4,1)S(1)} %fusion.2), kind=kOutput, calls=%fused_computation.2 | convolution fusion | flops 19365097472 | bytes 12622848 | tf_op jit(solution)/shard_map/dot_general | solution.py:55
  218.1 0.2 reshape.92
  218.3 0.9 copy.7
  219.2 8.9 %all-to-all-start.1 = ((f32[128,4,6]{2,1,0:T(4,128)}), f32[128,4,6]{2,1,0:T(4,128)S(1)}, u32[]{:S(2)}, u32[]{:S(2)}) async-start(f32[128,4,6]{2,1,0:T(4,128)} %copy.7), calls=%async_computation.1 | async-start | bytes 524288 | tf_op jit(solution)/shard_map/all_to_all | solution.py:62
  228.1 11.2 %all-to-all-done.1 = f32[128,4,6]{2,1,0:T(4,128)S(1)} async-done(((f32[128,4,6]{2,1,0:T(4,128)}), f32[128,4,6]{2,1,0:T(4,128)S(1)}, u32[]{:S(2)}, u32[]{:S(2)}) %all-to-all-start.1) | async-done | bytes 12320 | tf_op jit(solution)/shard_map/all_to_all | solution.py:62
  239.3 0.1 bitcast_reduce_fusion
  239.4 0.1 reshape.94
  239.5 3.4 %gather_fusion = f32[512]{0:T(512)} fusion(f32[768]{0:T(1024)S(1)} %reshape.94, s32[1024]{0:T(1024)S(1)} %pad_clamp_fusion), kind=kCustom, calls=%fused_computation | custom fusion | bytes 6144 | tf_op jit(solution)/shard_map/gather | solution.py:72
  (10 shorter events, 0.1 us)
Async XLA Ops:
  6.5 118.2 %all-gather.3.cloned.1.call-start = ((), (), s32[]{:S(2)}) async-start(), calls=%async_computation.2 | async-start | bytes 7864320 | tf_op jit(solution)/shard_map/all_gather | solution.py:44
  62.4 130.6 %all-gather.5.cloned.1.call-start = ((), (), s32[]{:S(2)}) async-start(), calls=%async_computation.3 | async-start | bytes 7864320 | tf_op jit(solution)/shard_map/all_gather | solution.py:43
  219.2 20.2 %all-to-all-start.1 = ((f32[128,4,6]{2,1,0:T(4,128)}), f32[128,4,6]{2,1,0:T(4,128)S(1)}, u32[]{:S(2)}, u32[]{:S(2)}) async-start(f32[128,4,6]{2,1,0:T(4,128)} %copy.7), calls=%async_computation.1 | async-start | bytes 524288 | tf_op jit(solution)/shard_map/all_to_all | solution.py:62
Sparse Core Ops, SparseCore 0:
  62.5 62.2 all-gather.2
  126.4 66.4 all-gather.4
